TPU v7x, 256 devices: a whole 4x4x8 slice. The times are simulated.
256 devices in a mesh: gz: 32 (over x, z_hi, core), ord: 8 (over y, z_lo).
Axes of the slice: x: 4, y: 4, z: 8 (z_hi: 4, z_lo: 2; z = z_hi * 2 + z_lo), core: 2. Of those that a mesh axis runs over, the one named last changes fastest.
Arguments:
- initial: float32 [96, 64, 128, 128], P('ord', 'gz'), may hold values from -1 to 1
- cotangent: float32 [96, 64, 128, 128], P('ord', 'gz'), may hold values from -6 to 6
- mobility: float32 [96], P('ord'), may hold values from 0.05 to 0.15
- stiffness: float32 [96], P('ord'), may hold values from 0.5 to 1
Outputs:
- adjoint_initial: float32 [96, 64, 128, 128], P('ord', 'gz')
All inputs are finite; a program needn't handle non-finite values.
Results may differ from a plain program's by a relative error of at most 0.00002.
Values sent between devices are 32-bit elements; how exact they have to be, the bound alone decides.
A program may use at most 128 MiB of HBM per device.

v0:
```python
import jax
import jax.numpy as jnp
from jax import lax
from jax.sharding import PartitionSpec as P

P_SIZE = 96
couple_scale = 2.0


def extended(block, sides, width):
    for axis, dim in sides:
        count = lax.axis_size(axis)
        forward = [(i, i + 1) for i in range(count - 1)]
        forward.append((count - 1, 0))
        backward = [(target, source) for source, target in forward]
        low = lax.ppermute(
            lax.slice_in_dim(block, block.shape[dim] - width, None, axis=dim), axis, forward
        )
        high = lax.ppermute(lax.slice_in_dim(block, 0, width, axis=dim), axis, backward)
        block = jnp.concatenate([low, block, high], axis=dim)
    return block


def inner_laplacian(values_ext):
    centre = values_ext[:, 1:-1]
    summed = values_ext[:, 2:] + values_ext[:, :-2] - 6.0 * centre
    for axis_num in (2, 3):
        summed = summed + jnp.roll(centre, 1, axis_num) + jnp.roll(centre, -1, axis_num)
    return summed


def well_slope(values, squares, coupling):
    return (
        -1.0 + 3.0 * values * values + 2.0 * coupling * squares - 6.0 * coupling * values * values
    )


def on_device(initial, cotangent, mobility, stiffness):
    order_dev = initial.shape[0]
    coupling = couple_scale / P_SIZE
    rate_col = mobility.reshape(-1, 1, 1, 1)
    stiff_col = stiffness.reshape(-1, 1, 1, 1)
    margin = 1
    joined = extended(jnp.concatenate((initial, cotangent), 0), (("gz", 1),), margin)
    field_ext = joined[:order_dev]
    adjoint_ext = joined[order_dev:]
    centre = field_ext[:, 1:-1]
    squares_first = lax.psum(jnp.sum(centre * centre, 0), "ord")
    potential = (
        -centre
        + centre * centre * centre
        + 2.0 * coupling * centre * (squares_first - centre * centre)
        - stiff_col * inner_laplacian(field_ext)
    )
    middle = centre - rate_col * potential
    scaled_ext = rate_col * adjoint_ext
    scaled = scaled_ext[:, 1:-1]
    squares_second, coupled_second = lax.psum(
        (jnp.sum(middle * middle, 0), jnp.sum(middle * scaled, 0)), "ord"
    )
    adjoint_middle = adjoint_ext[:, 1:-1] - (
        well_slope(middle, squares_second, coupling) * scaled
        + 4.0 * coupling * middle * coupled_second
        - stiff_col * inner_laplacian(scaled_ext)
    )
    scaled_middle = rate_col * adjoint_middle
    scaled_middle_ext = extended(scaled_middle, (("gz", 1),), 1)
    scaled_inner = scaled_middle_ext[:, 1:-1]
    coupled_first = lax.psum(jnp.sum(initial * scaled_inner, 0), "ord")
    return adjoint_middle - (
        well_slope(initial, squares_first, coupling) * scaled_inner
        + 4.0 * coupling * initial * coupled_first
        - stiff_col * inner_laplacian(scaled_middle_ext)
    )


def solution(mesh):
    return jax.shard_map(
        on_device,
        mesh=mesh,
        in_specs=(P("ord", "gz", None, None), P("ord", "gz", None, None), P("ord"), P("ord")),
        out_specs=P("ord", "gz", None, None),
        check_vma=False,
    )
```

profile of v0, /device:TPU:2, one launch (start us, length us, event | category | flops | bytes accessed | tf_op | source)
XLA Modules:
  0.0 316.3 jit_solution(2872398733217685041)
XLA Ops:
  6.5 0.0 copy-start.4
  6.5 0.0 all-reduce.5.cloned.1.call-start
  6.5 2.4 multiply_reduce_fusion
  9.0 0.0 copy-done.4
  9.0 0.1 constant_dynamic-update-slice_fusion
  9.1 0.0 copy-start.2
  9.1 0.0 copy-start
  9.1 1.9 fusion.47
  11.0 0.7 copy-done.2
  11.8 5.7 %collective-permute-start = (f32[24,1,128,128]{3,2,1,0:T(8,128)}, f32[24,1,128,128]{3,2,1,0:T(8,128)S(1)}, u32[]{:S(2)}, u32[]{:S(2)}) collective-permute-start(f32[24,1,128,128]{3,2,1,0:T(8,128)} %get-tuple-element.22), channel_id=1, source_target_pairs={{8,0},{16,8},{24,16},{32,24},{40,32},{48,40},{56,48},{64,56},{72,6... | collective-permute-start | bytes 4718600 | tf_op jit(solution)/shard_map/ppermute | solution.py:19
  17.5 0.0 collective-permute-start.1
  17.5 0.0 all-reduce.5.cloned.1.call-update
  17.5 0.0 all-reduce.9.cloned.1.call-start
  17.5 0.0 copy-done
  17.6 2.0 fusion.54
  19.5 2.2 fusion.55
  21.7 2.3 fusion.56
  24.0 86.5 %all-reduce.5.cloned.1.call-done = f32[2,128,128]{2,1,0:T(8,128)} async-done(((f32[2,128,128]{2,1,0:T(8,128)}), f32[2,128,128]{2,1,0:T(8,128)}) %all-reduce.5.cloned.1.call-update) | async-done | bytes 131088 | tf_op jit(solution)/shard_map/psum | solution.py:48
  110.5 0.9 broadcast_multiply_fusion.3
  111.4 0.0 collective-permute-done
  111.4 0.0 collective-permute-done.1
  111.4 0.0 copy-done.12
  111.4 0.0 copy-start.11
  111.5 2.1 fusion
  113.5 0.0 copy-start.1
  113.5 0.0 copy-start.7
  113.5 0.0 copy-start.8
  113.5 0.0 copy-start.9
  113.6 0.0 copy-start.10
  113.6 2.0 fusion.44
  115.5 0.0 copy-start.3
  115.5 0.0 copy-start.5
  115.5 0.0 copy-start.6
  115.5 2.2 fusion.45
  117.8 0.5 copy-done.1
  118.3 0.0 copy-done.11
  118.3 0.0 copy-done.7
  118.3 0.0 copy-done.8
  118.3 1.0 copy-done.9
  119.2 0.5 copy-done.10
  119.7 1.1 copy-done.3
  120.8 0.4 copy-done.5
  121.2 0.4 copy-done.6
  121.6 0.0 copy-done.13
  121.6 4.8 %multiply_reduce_fusion.3 = (f32[2,128,128]{2,1,0:T(8,128)}, f32[2,128,128]{2,1,0:T(8,128)}, f32[12,2,128,128]{3,2,1,0:T(8,128)}) fusion(f32[12,4,128,128]{3,2,1,0:T(8,128)S(1)} %fusion, f32[12,2,128,128]{3,2,1,0:T(8,128)S(1)} %copy-done, f32[12,2,128,1]{3,2,1,0:T(8,128)S(1)} %copy-done.8, f32[12,2,128,127]{3,2,1,0:T(8,128)S(1)} %copy-done.10, ...), kind=kLoop, calls=%fused_computation.57 | loop fusion | flops 11337728 | bytes 17694816 | tf_op jit(solution)/shard_map/reduce_sum | solution.py:59
  126.5 0.0 all-reduce.9.cloned.1.call-update
  126.5 0.0 all-reduce.7.cloned.1.call-start
  126.5 4.3 %fusion.46 = (f32[12,2,128,127]{3,2,1,0:T(8,128)}, f32[12,2,128,127]{3,2,1,0:T(8,128)}) fusion(f32[12,4,128,128]{3,2,1,0:T(8,128)} %copy-done.1), kind=kLoop, calls=%fused_computation.68 | loop fusion | bytes 6242304 | tf_op jit(solution)/shard_map/jit(_roll_static)/slice | solution.py:28
  130.8 1.0 fusion.43
  131.8 72.7 %all-reduce.9.cloned.1.call-done = (f32[2,128,128]{2,1,0:T(8,128)}, f32[2,128,128]{2,1,0:T(8,128)}) async-done(((f32[2,128,128]{2,1,0:T(8,128)}, f32[2,128,128]{2,1,0:T(8,128)}), (f32[2,128,128]{2,1,0:T(8,128)}, f32[2,128,128]{2,1,0:T(8,128)})) %all-reduce.9.cloned.1.call-update) | async-done | bytes 262160 | tf_op jit(solution)/shard_map/psum | solution.py:58
  204.5 1.0 broadcast_multiply_fusion.2
  205.5 8.8 %multiply_reduce_fusion.1 = (f32[2,128,128]{2,1,0:T(8,128)}, f32[12,2,128,128]{3,2,1,0:T(8,128)S(1)}, f32[12,2,128,128]{3,2,1,0:T(8,128)}) fusion(f32[12,2,128,128]{3,2,1,0:T(8,128)S(1)} %copy-done, f32[12]{0:T(128)S(1)} %copy-done.12, f32[12,2,128,128]{3,2,1,0:T(8,128)} %param.5, f32[12,2,128,1]{3,2,1,0:T(8,128)} %get-tuple-element.18, ...), kind=kLoop, calls=%fused_computation.55 | loop fusion | flops 10584064 | bytes 19267680 | tf_op jit(solution)/shard_map/reduce_sum | solution.py:69
  214.3 2.2 fusion.48
  216.5 2.2 fusion.49
  218.7 1.3 fusion.52
  220.0 0.0 collective-permute-start.2
  220.0 0.5 collective-permute-start.3
  220.5 0.0 all-reduce.7.cloned.1.call-update
  220.6 2.1 fusion.50
  222.7 79.8 %all-reduce.7.cloned.1.call-done = f32[2,128,128]{2,1,0:T(8,128)} async-done(((f32[2,128,128]{2,1,0:T(8,128)}), f32[2,128,128]{2,1,0:T(8,128)}) %all-reduce.7.cloned.1.call-update) | async-done | bytes 131088 | tf_op jit(solution)/shard_map/psum | solution.py:69
  302.5 0.9 broadcast_multiply_fusion.1
  303.4 0.0 collective-permute-done.2
  303.4 0.0 collective-permute-done.3
  303.4 6.4 %fusion.20 = f32[12,2,128,128]{3,2,1,0:T(8,128)} fusion(f32[12,2,128,128]{3,2,1,0:T(8,128)} %get-tuple-element.11, f32[12,2,128,128]{3,2,1,0:T(8,128)S(1)} %get-tuple-element.10, f32[12,2,128,128]{3,2,1,0:T(8,128)S(1)} %copy-done, f32[12,1,128,128]{3,2,1,0:T(8,128)} %collective-permute-done.3, f32[12,1,128,128]{3,2,1,0:T(8,128)} %collective-permute-done.2, ...), kind=kLoop, calls=%fused_computation.29 | loop fusion | flops 10223616 | bytes 14417968 | tf_op jit(solution)/shard_map/sub | solution.py:70
  (4 shorter events, 0.0 us)
Async XLA Ops:
  6.5 2.4 copy-start.4
  6.5 104.0 %all-reduce.5.cloned.1.call-start = ((), (), s32[]{:S(2)}) async-start(), calls=%async_computation | async-start | bytes 262144 | tf_op jit(solution)/shard_map/psum | solution.py:48
  9.1 2.7 copy-start.2
  9.1 8.4 %copy-start = (f32[12,2,128,128]{3,2,1,0:T(8,128)S(1)}, f32[12,2,128,128]{3,2,1,0:T(8,128)}, u32[]{:S(2)}) copy-start(f32[12,2,128,128]{3,2,1,0:T(8,128)} %param.4) | copy-start | bytes 4718596
  11.8 99.7 %collective-permute-start = (f32[24,1,128,128]{3,2,1,0:T(8,128)}, f32[24,1,128,128]{3,2,1,0:T(8,128)S(1)}, u32[]{:S(2)}, u32[]{:S(2)}) collective-permute-start(f32[24,1,128,128]{3,2,1,0:T(8,128)} %get-tuple-element.22), channel_id=1, source_target_pairs={{8,0},{16,8},{24,16},{32,24},{40,32},{48,40},{56,48},{64,56},{72,6... | collective-permute-start | bytes 4718600 | tf_op jit(solution)/shard_map/ppermute | solution.py:19
  17.5 94.0 %collective-permute-start.1 = (f32[24,1,128,128]{3,2,1,0:T(8,128)}, f32[24,1,128,128]{3,2,1,0:T(8,128)}, u32[]{:S(2)}, u32[]{:S(2)}) collective-permute-start(f32[24,1,128,128]{3,2,1,0:T(8,128)} %get-tuple-element.21), channel_id=1, source_target_pairs={{0,8},{8,16},{16,24},{24,32},{32,40},{40,48},{48,56},{56,64},{64,7... | collective-permute-start | bytes 4718600 | tf_op jit(solution)/shard_map/ppermute | solution.py:16
  17.5 187.0 %all-reduce.9.cloned.1.call-start = ((), (), s32[]{:S(2)}) async-start(), calls=%async_computation.2 | async-start | bytes 524288 | tf_op jit(solution)/shard_map/psum | solution.py:58
  21.7 89.7 %copy-start.12 = (f32[12]{0:T(128)S(1)}, f32[12]{0:T(128)}, u32[]{:S(2)}) copy-start(f32[12]{0:T(128)} %param.6) | copy-start | bytes 148
  111.4 6.8 %copy-start.11 = (f32[2,128,128]{2,1,0:T(8,128)S(1)}, f32[2,128,128]{2,1,0:T(8,128)}, u32[]{:S(2)}) copy-start(f32[2,128,128]{2,1,0:T(8,128)} %all-reduce.5.cloned.1.call-done) | copy-start | bytes 393220
  113.5 4.7 %copy-start.1 = (f32[12,4,128,128]{3,2,1,0:T(8,128)}, f32[12,4,128,128]{3,2,1,0:T(8,128)S(1)}, u32[]{:S(2)}) copy-start(f32[12,4,128,128]{3,2,1,0:T(8,128)S(1)} %fusion) | copy-start | bytes 9437188
  113.5 4.7 %copy-start.7 = (f32[12,2,128,1]{3,2,1,0:T(8,128)S(1)}, f32[12,2,128,1]{3,2,1,0:T(8,128)}, u32[]{:S(2)}) copy-start(f32[12,2,128,1]{3,2,1,0:T(8,128)} %get-tuple-element.39) | copy-start | bytes 36868
  113.5 4.7 %copy-start.8 = (f32[12,2,128,1]{3,2,1,0:T(8,128)S(1)}, f32[12,2,128,1]{3,2,1,0:T(8,128)}, u32[]{:S(2)}) copy-start(f32[12,2,128,1]{3,2,1,0:T(8,128)} %get-tuple-element.40) | copy-start | bytes 36868
  113.5 5.7 %copy-start.9 = (f32[12,2,128,127]{3,2,1,0:T(8,128)S(1)}, f32[12,2,128,127]{3,2,1,0:T(8,128)}, u32[]{:S(2)}) copy-start(f32[12,2,128,127]{3,2,1,0:T(8,128)} %get-tuple-element.41) | copy-start | bytes 4681732
  113.6 6.2 %copy-start.10 = (f32[12,2,128,127]{3,2,1,0:T(8,128)S(1)}, f32[12,2,128,127]{3,2,1,0:T(8,128)}, u32[]{:S(2)}) copy-start(f32[12,2,128,127]{3,2,1,0:T(8,128)} %get-tuple-element.42) | copy-start | bytes 4681732
  115.5 5.2 %copy-start.3 = (f32[24,2,128,128]{3,2,1,0:T(8,128)S(1)}, f32[24,2,128,128]{3,2,1,0:T(8,128)}, u32[]{:S(2)}) copy-start(f32[24,2,128,128]{3,2,1,0:T(8,128)} %copy-done.2) | copy-start | bytes 9437188
  115.5 5.7 %copy-start.5 = (f32[12,2,127,128]{3,2,1,0:T(8,128)S(1)}, f32[12,2,127,128]{3,2,1,0:T(8,128)}, u32[]{:S(2)}) copy-start(f32[12,2,127,128]{3,2,1,0:T(8,128)} %get-tuple-element.37) | copy-start | bytes 4681732
  115.5 6.1 %copy-start.6 = (f32[12,2,127,128]{3,2,1,0:T(8,128)S(1)}, f32[12,2,127,128]{3,2,1,0:T(8,128)}, u32[]{:S(2)}) copy-start(f32[12,2,127,128]{3,2,1,0:T(8,128)} %get-tuple-element.38) | copy-start | bytes 4681732
  115.5 6.1 %copy-start.13 = (f32[12]{0:T(128)S(1)}, f32[12]{0:T(128)}, u32[]{:S(2)}) copy-start(f32[12]{0:T(128)} %param.7) | copy-start | bytes 148
  126.5 176.0 %all-reduce.7.cloned.1.call-start = ((), (), s32[]{:S(2)}) async-start(), calls=%async_computation.1 | async-start | bytes 262144 | tf_op jit(solution)/shard_map/psum | solution.py:69
  220.0 83.3 %collective-permute-start.2 = (f32[12,1,128,128]{3,2,1,0:T(8,128)}, f32[12,1,128,128]{3,2,1,0:T(8,128)}, u32[]{:S(2)}, u32[]{:S(2)}) collective-permute-start(f32[12,1,128,128]{3,2,1,0:T(8,128)} %get-tuple-element.31), channel_id=1, source_target_pairs={{8,0},{16,8},{24,16},{32,24},{40,32},{48,40},{56,48},{64,56},{72,6... | collective-permute-start | bytes 2359304 | tf_op jit(solution)/shard_map/ppermute | solution.py:19
  220.0 83.4 %collective-permute-start.3 = (f32[12,1,128,128]{3,2,1,0:T(8,128)}, f32[12,1,128,128]{3,2,1,0:T(8,128)}, u32[]{:S(2)}, u32[]{:S(2)}) collective-permute-start(f32[12,1,128,128]{3,2,1,0:T(8,128)} %get-tuple-element.32), channel_id=1, source_target_pairs={{0,8},{8,16},{16,24},{24,32},{32,40},{40,48},{48,56},{56,64},{64,7... | collective-permute-start | bytes 2359304 | tf_op jit(solution)/shard_map/ppermute | solution.py:16
Sparse Core Ops, SparseCore 0:
  17.6 92.8 all-reduce.4
  126.6 77.8 all-reduce.8
  220.7 81.7 all-reduce.6
where the time goes:
time: 317 us; the launch traced here: 316 us
  waiting for transfers between devices  239 us (75%)
  local copies, waits for them, and re-layouts  30.3 us (10%)
  other arithmetic  27.4 us (9%)
  between operations  13.3 us (4%)
  starting transfers between devices  6.31 us (2%)
    psum x1, waiting for transfers between devices, on_device(): squares_first = lax.psum(jnp.sum(centre * centre, 0), 'ord')  86.5 us
    psum x1, waiting for transfers between devices, on_device(): coupled_first = lax.psum(jnp.sum(initial * scaled_inner, 0), 'ord')  79.8 us
    psum x1, waiting for transfers between devices, on_device(): lax.psum((jnp.sum(middle * middle, 0), jnp.sum(middle * scaled, 0)), 'ord')  72.7 us
    slice x8, local copies, waits for them, and re-layouts, inner_laplacian(): jnp.roll(centre, 1, axis_num)  15.9 us
    reduce_sum x1, other arithmetic, on_device(): coupled_first = lax.psum(jnp.sum(initial * scaled_inner, 0), 'ord')  8.83 us
    slice x4, local copies, waits for them, and re-layouts, inner_laplacian(): jnp.roll(centre, -1, axis_num)  6.48 us
    sub x1, other arithmetic, on_device(): adjoint_middle - (well_slope(initial, squares_first, coupling) * scaled_i...  6.4 us
  transfers between devices with their start and end apart: 7, of which 3 were waited for; matrix products, arithmetic and copies ran while one was open for 5% of the time, Pallas kernels for 0%

commit v1 on v0

--- a/solution.py
+++ b/solution.py
@@ -2,6 +2,7 @@
 import jax.numpy as jnp
 from jax import lax
 from jax.sharding import PartitionSpec as P
+from jax.lax import all_gather
 
 P_SIZE = 96
 couple_scale = 2.0
@@ -45,7 +46,11 @@
     field_ext = joined[:order_dev]
     adjoint_ext = joined[order_dev:]
     centre = field_ext[:, 1:-1]
-    squares_first = lax.psum(jnp.sum(centre * centre, 0), "ord")
+
+    def run_frames(in_array):
+        return jnp.sum(all_gather(in_array, "ord"), axis=0)
+
+    squares_first = run_frames(jnp.sum(centre * centre, 0))
     potential = (
         -centre
         + centre * centre * centre

time: 317 us -> 278 us (0.88)
  waiting for transfers between devices: 239 us -> 203 us
  local copies, waits for them, and re-layouts: 30.3 us -> 24.9 us
    psum x1 -> x0, waiting for transfers between devices: 86.5 us -> none  [on_device(): squares_first = lax.psum(jnp.sum(centre * centre, 0), 'ord')]
    ppermute x2, waiting for transfers between devices: 0.01 us -> 23.9 us  [extended(): lax.ppermute(lax.slice_in_dim(block, block.shape[dim] - width, None, axis...]
    ppermute x2, waiting for transfers between devices: 0.01 us -> 20.9 us  [extended(): lax.ppermute(lax.slice_in_dim(block, 0, width, axis=dim), axis, backward)]
    psum x1, waiting for transfers between devices: 72.7 us -> 78.7 us  [on_device(): lax.psum((jnp.sum(middle * middle, 0), jnp.sum(middle * scaled, 0)), 'ord')]
    unnamed x28 -> x14, local copies, waits for them, and re-layouts: 4.65 us -> 0.79 us
  transfers between devices with their start and end apart: 7 -> 7, of which waited for: 3 -> 4; matrix products, arithmetic and copies ran while one was open for 5% -> 7% of each run, Pallas kernels for 0% -> 0%
where the time goes in v1:
time: 278 us
  waiting for transfers between devices  203 us (73%)
  other arithmetic  30 us (11%)
  local copies, waits for them, and re-layouts  24.9 us (9%)
  between operations  13.2 us (5%)
  starting transfers between devices  6.31 us (2%)
    psum x1, waiting for transfers between devices, on_device(): coupled_first = lax.psum(jnp.sum(initial * scaled_inner, 0), 'ord')  79.8 us
    psum x1, waiting for transfers between devices, on_device(): lax.psum((jnp.sum(middle * middle, 0), jnp.sum(middle * scaled, 0)), 'ord')  78.7 us
    ppermute x2, waiting for transfers between devices, extended(): lax.ppermute(lax.slice_in_dim(block, block.shape[dim] - width, None, axis...  23.9 us
    ppermute x2, waiting for transfers between devices, extended(): lax.ppermute(lax.slice_in_dim(block, 0, width, axis=dim), axis, backward)  20.9 us
    slice x8, local copies, waits for them, and re-layouts, inner_laplacian(): jnp.roll(centre, 1, axis_num)  14.3 us
    reduce_sum x1, other arithmetic, on_device(): coupled_first = lax.psum(jnp.sum(initial * scaled_inner, 0), 'ord')  8.83 us
    reduce_sum x1, other arithmetic, on_device(): jnp.sum(middle * middle, 0)  7.51 us
    slice x4, local copies, waits for them, and re-layouts, inner_laplacian(): jnp.roll(centre, -1, axis_num)  6.42 us
  transfers between devices with their start and end apart: 7, of which 4 were waited for; matrix products, arithmetic and copies ran while one was open for 7% of the time, Pallas kernels for 0%

profile of v1, /device:TPU:2, one launch (start us, length us, event | category | flops | bytes accessed | tf_op | source)
XLA Modules:
  0.0 277.8 jit_solution(11100177016406118229)
XLA Ops:
  6.5 0.0 copy-start.4
  6.5 0.0 all-gather.3.cloned.1.call-start
  6.5 2.4 multiply_reduce_fusion
  9.0 0.0 copy-done.4
  9.0 0.1 constant_dynamic-update-slice_fusion
  9.1 0.0 copy-start.2
  9.1 0.0 copy-start
  9.1 1.9 fusion.47
  11.0 0.8 copy-done.2
  11.8 5.7 %collective-permute-start = (f32[24,1,128,128]{3,2,1,0:T(8,128)}, f32[24,1,128,128]{3,2,1,0:T(8,128)S(1)}, u32[]{:S(2)}, u32[]{:S(2)}) collective-permute-start(f32[24,1,128,128]{3,2,1,0:T(8,128)} %get-tuple-element.22), channel_id=1, source_target_pairs={{8,0},{16,8},{24,16},{32,24},{40,32},{48,40},{56,48},{64,56},{72,6... | collective-permute-start | bytes 4718600 | tf_op jit(solution)/shard_map/ppermute | solution.py:20
  17.5 0.0 collective-permute-start.1
  17.5 0.0 all-gather.3.cloned.1.call-update
  17.5 0.0 all-reduce.6.cloned.1.call-start
  17.6 0.0 copy-done
  17.6 2.0 fusion.54
  19.6 2.2 fusion.55
  21.8 0.0 copy-start.3
  21.8 0.0 copy-start.5
  21.8 2.2 fusion.56
  24.1 20.9 %collective-permute-done = f32[24,1,128,128]{3,2,1,0:T(8,128)S(1)} collective-permute-done((f32[24,1,128,128]{3,2,1,0:T(8,128)}, f32[24,1,128,128]{3,2,1,0:T(8,128)S(1)}, u32[]{:S(2)}, u32[]{:S(2)}) %collective-permute-start) | collective-permute-done | bytes 1572896 | tf_op jit(solution)/shard_map/ppermute | solution.py:20
  45.0 23.9 %collective-permute-done.1 = f32[24,1,128,128]{3,2,1,0:T(8,128)} collective-permute-done((f32[24,1,128,128]{3,2,1,0:T(8,128)}, f32[24,1,128,128]{3,2,1,0:T(8,128)}, u32[]{:S(2)}, u32[]{:S(2)}) %collective-permute-start.1) | collective-permute-done | bytes 1572896 | tf_op jit(solution)/shard_map/ppermute | solution.py:17
  68.8 0.0 copy-done.3
  68.8 0.0 copy-done.5
  68.9 1.6 fusion
  70.5 0.0 copy-start.1
  70.5 2.3 fusion.44
  72.8 2.2 fusion.45
  75.0 0.0 copy-done.1
  75.0 0.0 copy-start.6
  75.0 2.3 fusion.46
  77.3 0.0 all-gather.3.cloned.1.call-done
  77.3 1.3 reduce_sum.46
  78.6 0.0 copy-done.6
  78.6 7.5 %multiply_reduce_fusion.3 = (f32[2,128,128]{2,1,0:T(8,128)}, f32[2,128,128]{2,1,0:T(8,128)}, f32[12,2,128,128]{3,2,1,0:T(8,128)}) fusion(f32[12,4,128,128]{3,2,1,0:T(8,128)} %copy-done.1, f32[12,2,128,128]{3,2,1,0:T(8,128)S(1)} %copy-done, f32[12,2,128,1]{3,2,1,0:T(8,128)} %get-tuple-element.40, f32[12,2,128,127]{3,2,1,0:T(8,128)} %get-tuple-element.42, ...), kind=kLoop, calls=%fused_computation.57 | loop fusion | flops 11337728 | bytes 17694816 | tf_op jit(solution)/shard_map/reduce_sum | solution.py:64
  86.2 0.0 all-reduce.6.cloned.1.call-update
  86.2 0.0 all-reduce.4.cloned.1.call-start
  86.2 1.0 fusion.43
  87.2 78.7 %all-reduce.6.cloned.1.call-done = (f32[2,128,128]{2,1,0:T(8,128)}, f32[2,128,128]{2,1,0:T(8,128)}) async-done(((f32[2,128,128]{2,1,0:T(8,128)}, f32[2,128,128]{2,1,0:T(8,128)}), (f32[2,128,128]{2,1,0:T(8,128)}, f32[2,128,128]{2,1,0:T(8,128)})) %all-reduce.6.cloned.1.call-update) | async-done | bytes 262160 | tf_op jit(solution)/shard_map/psum | solution.py:63
  166.0 1.0 broadcast_multiply_fusion.2
  167.0 8.8 %multiply_reduce_fusion.1 = (f32[2,128,128]{2,1,0:T(8,128)}, f32[12,2,128,128]{3,2,1,0:T(8,128)S(1)}, f32[12,2,128,128]{3,2,1,0:T(8,128)}) fusion(f32[12,2,128,128]{3,2,1,0:T(8,128)S(1)} %copy-done, f32[12]{0:T(128)S(1)} %copy-done.5, f32[12,2,128,128]{3,2,1,0:T(8,128)} %param.5, f32[12,2,128,1]{3,2,1,0:T(8,128)} %get-tuple-element.18, ...), kind=kLoop, calls=%fused_computation.55 | loop fusion | flops 10584064 | bytes 19267680 | tf_op jit(solution)/shard_map/reduce_sum | solution.py:74
  175.8 2.2 fusion.48
  178.0 2.2 fusion.49
  180.2 1.3 fusion.52
  181.5 0.0 collective-permute-start.2
  181.5 0.5 collective-permute-start.3
  182.0 0.0 all-reduce.4.cloned.1.call-update
  182.0 2.0 fusion.50
  184.1 79.8 %all-reduce.4.cloned.1.call-done = f32[2,128,128]{2,1,0:T(8,128)} async-done(((f32[2,128,128]{2,1,0:T(8,128)}), f32[2,128,128]{2,1,0:T(8,128)}) %all-reduce.4.cloned.1.call-update) | async-done | bytes 131088 | tf_op jit(solution)/shard_map/psum | solution.py:74
  263.9 0.9 broadcast_multiply_fusion.1
  264.8 0.0 collective-permute-done.2
  264.8 0.0 collective-permute-done.3
  264.9 6.4 %fusion.20 = f32[12,2,128,128]{3,2,1,0:T(8,128)} fusion(f32[12,2,128,128]{3,2,1,0:T(8,128)} %get-tuple-element.11, f32[12,2,128,128]{3,2,1,0:T(8,128)S(1)} %get-tuple-element.10, f32[12,2,128,128]{3,2,1,0:T(8,128)S(1)} %copy-done, f32[12,1,128,128]{3,2,1,0:T(8,128)} %collective-permute-done.3, f32[12,1,128,128]{3,2,1,0:T(8,128)} %collective-permute-done.2, ...), kind=kLoop, calls=%fused_computation.29 | loop fusion | flops 10223616 | bytes 14417968 | tf_op jit(solution)/shard_map/sub | solution.py:75
  (3 shorter events, 0.1 us)
Async XLA Ops:
  6.5 2.4 copy-start.4
  6.5 70.8 %all-gather.3.cloned.1.call-start = ((), (), s32[]{:S(2)}) async-start(), calls=%async_computation.1 | async-start | bytes 1179648 | tf_op jit(solution)/shard_map/all_gather | solution.py:51
  9.1 2.7 copy-start.2
  9.1 8.5 %copy-start = (f32[12,2,128,128]{3,2,1,0:T(8,128)S(1)}, f32[12,2,128,128]{3,2,1,0:T(8,128)}, u32[]{:S(2)}) copy-start(f32[12,2,128,128]{3,2,1,0:T(8,128)} %param.4) | copy-start | bytes 4718596
  11.8 33.2 %collective-permute-start = (f32[24,1,128,128]{3,2,1,0:T(8,128)}, f32[24,1,128,128]{3,2,1,0:T(8,128)S(1)}, u32[]{:S(2)}, u32[]{:S(2)}) collective-permute-start(f32[24,1,128,128]{3,2,1,0:T(8,128)} %get-tuple-element.22), channel_id=1, source_target_pairs={{8,0},{16,8},{24,16},{32,24},{40,32},{48,40},{56,48},{64,56},{72,6... | collective-permute-start | bytes 4718600 | tf_op jit(solution)/shard_map/ppermute | solution.py:20
  17.5 51.4 %collective-permute-start.1 = (f32[24,1,128,128]{3,2,1,0:T(8,128)}, f32[24,1,128,128]{3,2,1,0:T(8,128)}, u32[]{:S(2)}, u32[]{:S(2)}) collective-permute-start(f32[24,1,128,128]{3,2,1,0:T(8,128)} %get-tuple-element.21), channel_id=1, source_target_pairs={{0,8},{8,16},{16,24},{24,32},{32,40},{40,48},{48,56},{56,64},{64,7... | collective-permute-start | bytes 4718600 | tf_op jit(solution)/shard_map/ppermute | solution.py:17
  17.5 148.5 %all-reduce.6.cloned.1.call-start = ((), (), s32[]{:S(2)}) async-start(), calls=%async_computation.2 | async-start | bytes 524288 | tf_op jit(solution)/shard_map/psum | solution.py:63
  21.8 47.0 %copy-start.3 = (f32[24,2,128,128]{3,2,1,0:T(8,128)S(1)}, f32[24,2,128,128]{3,2,1,0:T(8,128)}, u32[]{:S(2)}) copy-start(f32[24,2,128,128]{3,2,1,0:T(8,128)} %copy-done.2) | copy-start | bytes 9437188
  21.8 47.0 %copy-start.5 = (f32[12]{0:T(128)S(1)}, f32[12]{0:T(128)}, u32[]{:S(2)}) copy-start(f32[12]{0:T(128)} %param.6) | copy-start | bytes 148
  70.5 4.6 %copy-start.1 = (f32[12,4,128,128]{3,2,1,0:T(8,128)}, f32[12,4,128,128]{3,2,1,0:T(8,128)S(1)}, u32[]{:S(2)}) copy-start(f32[12,4,128,128]{3,2,1,0:T(8,128)S(1)} %fusion) | copy-start | bytes 9437188
  75.0 3.6 %copy-start.6 = (f32[12]{0:T(128)S(1)}, f32[12]{0:T(128)}, u32[]{:S(2)}) copy-start(f32[12]{0:T(128)} %param.7) | copy-start | bytes 148
  86.2 177.7 %all-reduce.4.cloned.1.call-start = ((), (), s32[]{:S(2)}) async-start(), calls=%async_computation | async-start | bytes 262144 | tf_op jit(solution)/shard_map/psum | solution.py:74
  181.5 83.3 %collective-permute-start.2 = (f32[12,1,128,128]{3,2,1,0:T(8,128)}, f32[12,1,128,128]{3,2,1,0:T(8,128)}, u32[]{:S(2)}, u32[]{:S(2)}) collective-permute-start(f32[12,1,128,128]{3,2,1,0:T(8,128)} %get-tuple-element.31), channel_id=1, source_target_pairs={{8,0},{16,8},{24,16},{32,24},{40,32},{48,40},{56,48},{64,56},{72,6... | collective-permute-start | bytes 2359304 | tf_op jit(solution)/shard_map/ppermute | solution.py:20
  181.5 83.4 %collective-permute-start.3 = (f32[12,1,128,128]{3,2,1,0:T(8,128)}, f32[12,1,128,128]{3,2,1,0:T(8,128)}, u32[]{:S(2)}, u32[]{:S(2)}) collective-permute-start(f32[12,1,128,128]{3,2,1,0:T(8,128)} %get-tuple-element.32), channel_id=1, source_target_pairs={{0,8},{8,16},{16,24},{24,32},{32,40},{40,48},{48,56},{56,64},{64,7... | collective-permute-start | bytes 2359304 | tf_op jit(solution)/shard_map/ppermute | solution.py:17
Sparse Core Ops, SparseCore 0:
  17.6 59.4 all-gather.2
  86.3 79.6 all-reduce.5
  182.1 81.7 all-reduce.3
